TPU v7x, 128 devices: a whole 4x4x4 slice. The times are simulated.
128 devices in a mesh: gx: 32 (over y, z, x_lo), gy: 4 (over x_hi, core).
Axes of the slice: x: 4 (x_hi: 2, x_lo: 2; x = x_hi * 2 + x_lo), y: 4, z: 4, core: 2. Of those that a mesh axis runs over, the one named last changes fastest.
Arguments:
- right_side: float32 [2, 2048, 256, 128], P(None, 'gx', 'gy'), may hold values from -8 to 8
- well_coef: float32 [2048, 256, 128], P('gx', 'gy'), may hold values from 2 to 6
- mobility_coef: float32 [2048, 256, 128], P('gx', 'gy'), may hold values from 2 to 6
- coupling: float32 [2048, 256, 128], P('gx', 'gy'), may hold values from -0.5 to 0.5
- phase_old: float32 [2048, 256, 128], P('gx', 'gy'), may hold values from -1 to 1
- unit_owner: int32 [16384], P(('gx', 'gy')), may hold values from 0 to 127, as said below
- velocity: float32 [3, 16384, 512], P(None, ('gx', 'gy')), may hold values from -4 to 4
Outputs:
- correction: float32 [2, 2048, 256, 128], P(None, 'gx', 'gy')
- momentum: float32 [3, 16384, 512], P(None, ('gx', 'gy'))
Inputs may be any that keep to these rules, and one draw needn't show every extreme that they name: `unit_owner`: each device's 128 units go to 128 different owners, and every owner receives exactly one unit from each device.
All inputs are finite; a program needn't handle non-finite values.
Results may differ from a plain program's by a relative error of at most 0.000088.
Values sent between devices are 32-bit elements; how exact they have to be, the bound alone decides.
A program may use at most 128 MiB of HBM per device.

v0:
```python
import functools

import jax
import jax.numpy as jnp
from jax import lax
from jax.experimental import pallas as pl
from jax.experimental.pallas import tpu as pltpu
from jax.sharding import PartitionSpec as P

SWEEPS = 3
LOW_BOUND = 0.15
HIGH_BOUND = 1.85
THETA = (HIGH_BOUND + LOW_BOUND) / 2.0
DELTA = (HIGH_BOUND - LOW_BOUND) / 2.0
SIGMA = THETA / DELTA

PAD = 8
MESH = pl.DeviceIdType.MESH


def recurrence():
    out = []
    rho = 1.0 / SIGMA
    decay_before, gain_before = 0.0, 0.0
    for sweep in range(SWEEPS):
        rho_new = 1.0 / (2.0 * SIGMA - rho)
        decay, gain = rho_new * rho, 2.0 * rho_new / DELTA
        if sweep == 0:
            out.append((decay + gain * (THETA - 1.0), 0.0, gain))
        else:
            ratio = gain / gain_before
            out.append((decay + ratio - gain, -ratio * decay_before, gain))
        decay_before, gain_before, rho = decay, gain, rho_new
    return out


def kernel_body(
    sizes,
    order,
    rhs_hbm,
    well_hbm,
    mob_hbm,
    cpl_hbm,
    pold_hbm,
    vel_hbm,
    corr_hbm,
    mom_hbm,
    rhs,
    inv,
    cpl,
    pold,
    dir0,
    dir1,
    dir2,
    phase,
    slab,
    packed,
    stage,
    recv,
    vel,
    mom,
    load_sem,
    rest_sem,
    out_sem,
    halo_send,
    halo_recv,
    unit_send,
    unit_recv,
):
    ngx, ngy, cx, cy, cz, chunks = sizes
    ndev = ngx * ngy
    gx, gy = lax.axis_index("gx"), lax.axis_index("gy")
    me = gx * ngy + gy
    per = cx // chunks
    lo, hi = PAD, PAD + cy
    unit_rows = packed.shape[1]

    def load_chunk(i):
        at = pl.ds(i * per, per)
        return (
            pltpu.make_async_copy(rhs_hbm.at[:, at], rhs.at[:, at], load_sem.at[i, 0]),
            pltpu.make_async_copy(well_hbm.at[at], inv.at[0, at], load_sem.at[i, 1]),
            pltpu.make_async_copy(mob_hbm.at[at], inv.at[1, at], load_sem.at[i, 2]),
        )

    load_cpl = pltpu.make_async_copy(cpl_hbm, cpl, rest_sem.at[0])
    load_pold = pltpu.make_async_copy(pold_hbm, pold, rest_sem.at[1])
    load_vel = pltpu.make_async_copy(vel_hbm, vel, rest_sem.at[2])
    chunk_order = [0, chunks - 1] + list(range(1, chunks - 1))
    for i in chunk_order:
        for copy in load_chunk(i):
            copy.start()
    load_cpl.start()
    load_pold.start()
    load_vel.start()

    for buf in (dir0, dir1, dir2):
        @pl.when(gx == 0)
        def _(buf=buf):
            buf[:, 0, lo:hi, :] = jnp.zeros((2, cy, cz), jnp.float32)

        @pl.when(gx == ngx - 1)
        def _(buf=buf):
            buf[:, cx + 1, lo:hi, :] = jnp.zeros((2, cy, cz), jnp.float32)

        @pl.when(gy == 0)
        def _(buf=buf):
            buf[:, 1 : cx + 1, lo - 1 : lo, :] = jnp.zeros((2, cx, 1, cz), jnp.float32)

        @pl.when(gy == ngy - 1)
        def _(buf=buf):
            buf[:, 1 : cx + 1, hi : hi + 1, :] = jnp.zeros((2, cx, 1, cz), jnp.float32)

    @pl.when(gx == 0)
    def _():
        phase[0, lo:hi, :] = jnp.zeros((cy, cz), jnp.float32)

    @pl.when(gx == ngx - 1)
    def _():
        phase[cx + 1, lo:hi, :] = jnp.zeros((cy, cz), jnp.float32)

    @pl.when(gy == 0)
    def _():
        phase[1 : cx + 1, lo - 1 : lo, :] = jnp.zeros((cx, 1, cz), jnp.float32)

    @pl.when(gy == ngy - 1)
    def _():
        phase[1 : cx + 1, hi : hi + 1, :] = jnp.zeros((cx, 1, cz), jnp.float32)

    def halo_copy(step, ref, way):
        lead = (slice(None),) if len(ref.shape) == 4 else ()
        own, rows = slice(lo, hi), slice(1, cx + 1)
        src, dst, target = (
            ((1, own), (cx + 1, own), (gx - 1, gy)),
            ((cx, own), (0, own), (gx + 1, gy)),
            ((rows, slice(lo, lo + 1)), (rows, slice(hi, hi + 1)), (gx, gy - 1)),
            ((rows, slice(hi - 1, hi)), (rows, slice(lo - 1, lo)), (gx, gy + 1)),
        )[way]
        return pltpu.make_async_remote_copy(
            src_ref=ref.at[lead + src],
            dst_ref=ref.at[lead + dst],
            send_sem=halo_send.at[step, way],
            recv_sem=halo_recv.at[step, way],
            device_id=target,
            device_id_type=MESH,
        )

    sends = (gx > 0, gx < ngx - 1, gy > 0, gy < ngy - 1)
    receives = (gx < ngx - 1, gx > 0, gy < ngy - 1, gy > 0)

    def send(step, ref, ways):
        for way in ways:

            @pl.when(sends[way])
            def _(way=way):
                halo_copy(step, ref, way).start()

    def receive(step, ref):
        for way in range(4):

            @pl.when(receives[way])
            def _(way=way):
                halo_copy(step, ref, way).wait_recv()

    def finish(step, ref):
        for way in range(4):

            @pl.when(sends[way])
            def _(way=way):
                halo_copy(step, ref, way).wait_send()

    lane = lax.broadcasted_iota(jnp.int32, (1, cz), 1)
    first_lane, last_lane = lane == 0, lane == cz - 1

    def along_depth(v):
        before = jnp.where(first_lane, 0.0, pltpu.roll(v, 1, axis=1))
        after = jnp.where(last_lane, 0.0, pltpu.roll(v, cz - 1, axis=1))
        return before, after

    def start_plane(x):
        for c in range(2):
            part = 1.0 / (inv[c, x] + 6.0)
            inv[c, x] = part
            dir0[c, x + 1, lo:hi, :] = part * rhs[c, x] * (1.0 / THETA)

    for n, i in enumerate(chunk_order):
        for copy in load_chunk(i):
            copy.wait()
        lax.fori_loop(i * per, (i + 1) * per, lambda x, _: (start_plane(x), 0)[1], 0)
        if n == 1:
            send(0, dir0, (0, 1))
    send(0, dir0, (2, 3))
    load_cpl.wait()

    table = recurrence()

    def sweep_rows(sweep, x, y, rows):
        now = (dir0, dir1, dir2)[sweep]
        of_now, of_before, of_update = table[sweep]
        at = pl.ds(lo + y, rows)
        mid = [now[c, x + 1, at, :] for c in range(2)]
        mix = cpl[x, pl.ds(y, rows), :]
        out = []
        for c in range(2):
            before, after = along_depth(mid[c])
            nbrs = now[c, x, at, :] + now[c, x + 2, at, :]
            nbrs = nbrs + now[c, x + 1, pl.ds(lo + y - 1, rows), :]
            nbrs = nbrs + now[c, x + 1, pl.ds(lo + y + 1, rows), :]
            nbrs = nbrs + (before + after)
            update = inv[c, x, pl.ds(y, rows), :] * (nbrs - mix * mid[1 - c])
            new = of_now * mid[c] + of_update * update
            if sweep > 0:
                new = new + of_before * (dir0, dir1)[sweep - 1][c, x + 1, at, :]
            out.append(new)
        if sweep < SWEEPS - 1:
            for c in range(2):
                (dir1, dir2)[sweep][c, x + 1, at, :] = out[c]
        else:
            for c in range(2):
                total = dir0[c, x + 1, at, :] + dir1[c, x + 1, at, :]
                total = total + mid[c] + out[c]
                rhs[c, x, pl.ds(y, rows), :] = total
                if c == 0:
                    phase[x + 1, at, :] = pold[x, pl.ds(y, rows), :] + total

    for sweep in range(SWEEPS):
        now = (dir0, dir1, dir2)[sweep]
        new = (dir1, dir2, phase)[sweep]
        receive(sweep, now)
        if sweep == SWEEPS - 1:
            load_pold.wait()
        sweep_rows(sweep, 0, 0, cy)
        sweep_rows(sweep, cx - 1, 0, cy)
        send(sweep + 1, new, (0, 1))

        def edges(x, _, sweep=sweep):
            sweep_rows(sweep, x, 0, 8)
            sweep_rows(sweep, x, cy - 8, 8)
            return 0

        lax.fori_loop(1, cx - 1, edges, 0)
        send(sweep + 1, new, (2, 3))

        def inner(x, _, sweep=sweep):
            sweep_rows(sweep, x, 8, cy - 16)
            return 0

        lax.fori_loop(1, cx - 1, inner, 0)

    store_corr = pltpu.make_async_copy(rhs, corr_hbm, out_sem.at[0])
    store_corr.start()
    receive(SWEEPS, phase)

    deep = lax.broadcasted_iota(jnp.int32, (2 * cz, cz), 0) // 2
    wide = lax.broadcasted_iota(jnp.int32, (2 * cz, cz), 1)
    pairing = jnp.where(deep == wide, 0.125, 0.0).astype(jnp.float32)

    def coarse_plane(i, _):
        sums = [None] * 4
        for x in (2 * i, 2 * i + 1):
            at = pl.ds(lo, cy)
            mid = phase[x + 1, at, :]
            half = 0.5 * rhs[1, x]
            before, after = along_depth(mid)
            fields = (
                mid,
                half * (phase[x + 2, at, :] - phase[x, at, :]),
                half * (phase[x + 1, pl.ds(lo + 1, cy), :] - phase[x + 1, pl.ds(lo - 1, cy), :]),
                half * (after - before),
            )
            sums = [f if s is None else s + f for s, f in zip(sums, fields)]
        for f in range(4):
            slab[f] = sums[f]
        rows = []
        quarter = cy // 4
        for f in range(4):
            part = [slab[f, pl.ds(k, quarter, stride=4), :] for k in range(4)]
            rows.append(jnp.concatenate([part[0] + part[1], part[2] + part[3]], axis=1))
        both = jnp.concatenate(rows, axis=0)
        mean = jnp.dot(
            both, pairing, precision=lax.Precision.HIGHEST, preferred_element_type=jnp.float32
        )
        for f in range(4):
            for q in range(4):
                base = f * quarter + q * 4
                packed[i * 4 + q, f * 4 : f * 4 + 4, :] = mean[base : base + 4, :]
        return 0

    lax.fori_loop(0, cx // 2, coarse_plane, 0)

    def unit_copy(peer):
        return pltpu.make_async_remote_copy(
            src_ref=stage.at[peer],
            dst_ref=recv.at[pl.ds(me * unit_rows, unit_rows)],
            send_sem=unit_send,
            recv_sem=unit_recv,
            device_id=(peer // ngy, peer % ngy),
            device_id_type=MESH,
        )

    def ship(k, _):
        peer = lax.rem(me + k, ndev)
        stage[peer] = packed[order[peer]]
        unit_copy(peer).start()
        return 0

    lax.fori_loop(1, ndev, ship, 0)
    recv[pl.ds(me * unit_rows, unit_rows), :] = packed[order[me]]

    for step, ref in enumerate((dir0, dir1, dir2, phase)):
        finish(step, ref)
    load_vel.wait()
    others = pl.ds(0, (ndev - 1) * unit_rows)
    pltpu.make_async_copy(recv.at[others], recv.at[others], unit_recv).wait()

    place = lax.rem(lane, cz // 2)
    bottom, top = place == 0, place == cz // 2 - 1

    def product(v, density, visc, weight):
        below = jnp.where(bottom, 0.0, pltpu.roll(v, 1, axis=1))
        flux = weight * (v - below)
        above = jnp.where(top, -visc * v, pltpu.roll(flux, cz - 1, axis=1))
        return density * v - (above - flux)

    for r in range(4):
        get = lambda f: recv[pl.ds(f * 4 + r, ndev, stride=unit_rows), :]
        mean = get(0)
        density = 0.1 + 0.45 * (1.0 + mean)
        visc = 0.2 + 0.4 * (1.0 + mean)
        weight = 0.5 * (visc + jnp.where(bottom, visc, pltpu.roll(visc, 1, axis=1)))
        for c in range(3):
            at = pl.ds(r * cz, cz)
            stress = product(vel[c, :, at], density, visc, weight) - get(c + 1)
            mom[c, :, at] = product(stress, density, visc, weight)

    store_mom = pltpu.make_async_copy(mom, mom_hbm, out_sem.at[1])
    store_mom.start()
    sent = pl.ds(0, ndev - 1)
    pltpu.make_async_copy(stage.at[sent], stage.at[sent], unit_send).wait()
    store_corr.wait()
    store_mom.wait()


def body(ngx, ngy, right_side, well_coef, mobility_coef, coupling, phase_old, unit_owner, velocity):
    _, cx, cy, cz = right_side.shape
    ndev = ngx * ngy
    chunks = 8
    unit_rows = 4 * (velocity.shape[2] // cz)
    ids = jnp.arange(ndev, dtype=jnp.int32)
    order = jnp.sum(jnp.where(unit_owner[None, :] == ids[:, None], ids[None, :], 0), axis=1)
    any_spec = pl.BlockSpec(memory_space=pl.ANY)
    padded = (cx + 2, cy + 2 * PAD, cz)
    f32 = jnp.float32
    return pl.pallas_call(
        functools.partial(kernel_body, (ngx, ngy, cx, cy, cz, chunks)),
        out_shape=(
            jax.ShapeDtypeStruct(right_side.shape, f32),
            jax.ShapeDtypeStruct(velocity.shape, f32),
        ),
        in_specs=[pl.BlockSpec(memory_space=pltpu.SMEM)] + [any_spec] * 6,
        out_specs=(any_spec, any_spec),
        scratch_shapes=[
            pltpu.VMEM((2, cx, cy, cz), f32),
            pltpu.VMEM((2, cx, cy, cz), f32),
            pltpu.VMEM((cx, cy, cz), f32),
            pltpu.VMEM((cx, cy, cz), f32),
            pltpu.VMEM((2,) + padded, f32),
            pltpu.VMEM((2,) + padded, f32),
            pltpu.VMEM((2,) + padded, f32),
            pltpu.VMEM(padded, f32),
            pltpu.VMEM((4, cy, cz), f32),
            pltpu.VMEM((ndev, unit_rows, cz), f32),
            pltpu.VMEM((ndev, unit_rows, cz), f32),
            pltpu.VMEM((ndev * unit_rows, cz), f32),
            pltpu.VMEM(velocity.shape, f32),
            pltpu.VMEM(velocity.shape, f32),
            pltpu.SemaphoreType.DMA((chunks, 3)),
            pltpu.SemaphoreType.DMA((3,)),
            pltpu.SemaphoreType.DMA((2,)),
            pltpu.SemaphoreType.DMA((SWEEPS + 1, 4)),
            pltpu.SemaphoreType.DMA((SWEEPS + 1, 4)),
            pltpu.SemaphoreType.DMA,
            pltpu.SemaphoreType.DMA,
        ],
        compiler_params=pltpu.CompilerParams(
            has_side_effects=True, vmem_limit_bytes=56 * 1024 * 1024
        ),
    )(order, right_side, well_coef, mobility_coef, coupling, phase_old, velocity)


def solution(mesh):
    return jax.shard_map(
        functools.partial(body, mesh.shape["gx"], mesh.shape["gy"]),
        mesh=mesh,
        in_specs=(
            P(None, "gx", "gy", None),
            P("gx", "gy", None),
            P("gx", "gy", None),
            P("gx", "gy", None),
            P("gx", "gy", None),
            P(("gx", "gy")),
            P(None, ("gx", "gy"), None),
        ),
        out_specs=(P(None, "gx", "gy", None), P(None, ("gx", "gy"), None)),
        check_vma=False,
    )
```

profile of v0, /device:TPU:1, one launch (start us, length us, event | category | flops | bytes accessed | tf_op | source)
XLA Modules:
  0.0 92.7 jit_solution(13328308241712437555)
XLA Ops:
  0.6 1.3 %select_reduce_fusion.order = s32[128]{0:T(128)} fusion(s32[128]{0:T(128)} %param.12), kind=kLoop, calls=%fused_computation | loop fusion | flops 49024 | bytes 1024 | tf_op jit(solution)/shard_map/reduce_sum | solution.py:350
  1.9 85.0 %shard_map.86 = (f32[2,64,64,128]{3,2,1,0:T(8,128)}, f32[3,128,512]{2,1,0:T(8,128)}) custom-call(s32[128]{0:T(128)} %select_reduce_fusion.order, f32[2,64,64,128]{3,2,1,0:T(8,128)} %rhs_hbm.1, f32[64,64,128]{2,1,0:T(8,128)} %well_hbm.1, f32[64,64,128]{2,1,0:T(8,128)} %mob_hbm.1, f32[64,64,128]{2,1,0:T(8,128)} %cpl_hbm.1, f32[64,64,128]{2,1,0:T(8,128)} %pold_hbm.1, ...), custom_call_target="tpu_custom_call" | custom-call | tf_op jit(solution)/shard_map/pallas_call | solution.py:354
  87.0 0.0 copy-start
  87.0 4.9 %copy.11 = f32[2,64,64,128]{3,2,1,0:T(8,128)} copy(f32[2,64,64,128]{3,2,1,0:T(8,128)} %get-tuple-element.4) | data formatting | bytes 8388608
  91.8 0.0 copy-done
  91.8 0.9 copy.12
Async XLA Ops:
  87.0 4.9 %copy-start = (f32[3,128,512]{2,1,0:T(8,128)S(1)}, f32[3,128,512]{2,1,0:T(8,128)}, u32[]{:S(2)}) copy-start(f32[3,128,512]{2,1,0:T(8,128)} %get-tuple-element.5) | copy-start | bytes 2359300
where the time goes:
time: 92.8 us; the launch traced here: 92.7 us
  Pallas kernels  85 us (92%)
  local copies, waits for them, and re-layouts  5.74 us (6%)
  other arithmetic  1.28 us (1%)
    pallas_call x1, Pallas kernels, body(): pl.pallas_call(functools.partial(kernel_body, (ngx, ngy, cx, cy, cz, chun...  85 us
    unnamed x4, local copies, waits for them, and re-layouts  5.74 us

commit v1 on v0

--- a/solution.py
+++ b/solution.py
@@ -19,19 +19,21 @@
 
 
 def recurrence():
-    out = []
+    table, scales = [], [1.0]
     rho = 1.0 / SIGMA
     decay_before, gain_before = 0.0, 0.0
     for sweep in range(SWEEPS):
         rho_new = 1.0 / (2.0 * SIGMA - rho)
         decay, gain = rho_new * rho, 2.0 * rho_new / DELTA
         if sweep == 0:
-            out.append((decay + gain * (THETA - 1.0), 0.0, gain))
+            table.append(((decay + gain * (THETA - 1.0)) / gain, 0.0))
         else:
             ratio = gain / gain_before
-            out.append((decay + ratio - gain, -ratio * decay_before, gain))
+            before = -ratio * decay_before * scales[-2] / (gain * scales[-1])
+            table.append(((decay + ratio - gain) / gain, before))
+        scales.append(scales[-1] * gain)
         decay_before, gain_before, rho = decay, gain, rho_new
-    return out
+    return table, scales
 
 
 def kernel_body(
@@ -94,6 +96,17 @@
     load_pold.start()
     load_vel.start()
 
+    barrier = pltpu.get_barrier_semaphore()
+
+    def greet(k, _):
+        peer = lax.rem(me + k, ndev)
+        pl.semaphore_signal(
+            barrier, inc=1, device_id=(peer // ngy, lax.rem(peer, ngy)), device_id_type=MESH
+        )
+        return 0
+
+    lax.fori_loop(1, ndev, greet, 0)
+
     for buf in (dir0, dir1, dir2):
         @pl.when(gx == 0)
         def _(buf=buf):
@@ -177,6 +190,14 @@
         after = jnp.where(last_lane, 0.0, pltpu.roll(v, cz - 1, axis=1))
         return before, after
 
+    def planes(first, last, together, work):
+        def some(i, _):
+            for k in range(together):
+                work(first + i * together + k)
+            return 0
+
+        lax.fori_loop(0, (last - first) // together, some, 0)
+
     def start_plane(x):
         for c in range(2):
             part = 1.0 / (inv[c, x] + 6.0)
@@ -186,17 +207,18 @@
     for n, i in enumerate(chunk_order):
         for copy in load_chunk(i):
             copy.wait()
-        lax.fori_loop(i * per, (i + 1) * per, lambda x, _: (start_plane(x), 0)[1], 0)
-        if n == 1:
+        planes(i * per, (i + 1) * per, 4, start_plane)
+        if n == 4:
+            pl.semaphore_wait(barrier, ndev - 1)
             send(0, dir0, (0, 1))
     send(0, dir0, (2, 3))
     load_cpl.wait()
 
-    table = recurrence()
+    table, scales = recurrence()
 
     def sweep_rows(sweep, x, y, rows):
         now = (dir0, dir1, dir2)[sweep]
-        of_now, of_before, of_update = table[sweep]
+        of_now, of_before = table[sweep]
         at = pl.ds(lo + y, rows)
         mid = [now[c, x + 1, at, :] for c in range(2)]
         mix = cpl[x, pl.ds(y, rows), :]
@@ -208,7 +230,7 @@
             nbrs = nbrs + now[c, x + 1, pl.ds(lo + y + 1, rows), :]
             nbrs = nbrs + (before + after)
             update = inv[c, x, pl.ds(y, rows), :] * (nbrs - mix * mid[1 - c])
-            new = of_now * mid[c] + of_update * update
+            new = of_now * mid[c] + update
             if sweep > 0:
                 new = new + of_before * (dir0, dir1)[sweep - 1][c, x + 1, at, :]
             out.append(new)
@@ -217,8 +239,8 @@
                 (dir1, dir2)[sweep][c, x + 1, at, :] = out[c]
         else:
             for c in range(2):
-                total = dir0[c, x + 1, at, :] + dir1[c, x + 1, at, :]
-                total = total + mid[c] + out[c]
+                total = scales[0] * dir0[c, x + 1, at, :] + scales[1] * dir1[c, x + 1, at, :]
+                total = total + (scales[2] * mid[c] + scales[3] * out[c])
                 rhs[c, x, pl.ds(y, rows), :] = total
                 if c == 0:
                     phase[x + 1, at, :] = pold[x, pl.ds(y, rows), :] + total
@@ -233,60 +255,56 @@
         sweep_rows(sweep, cx - 1, 0, cy)
         send(sweep + 1, new, (0, 1))
 
-        def edges(x, _, sweep=sweep):
+        def edges(x, sweep=sweep):
             sweep_rows(sweep, x, 0, 8)
             sweep_rows(sweep, x, cy - 8, 8)
-            return 0
-
-        lax.fori_loop(1, cx - 1, edges, 0)
+
+        sweep_rows(sweep, cx - 2, 0, cy)
+        sweep_rows(sweep, cx - 3, 0, cy)
+        planes(1, cx - 3, 12, edges)
         send(sweep + 1, new, (2, 3))
-
-        def inner(x, _, sweep=sweep):
-            sweep_rows(sweep, x, 8, cy - 16)
-            return 0
-
-        lax.fori_loop(1, cx - 1, inner, 0)
+        planes(1, cx - 3, 6, lambda x, sweep=sweep: sweep_rows(sweep, x, 8, cy - 16))
 
     store_corr = pltpu.make_async_copy(rhs, corr_hbm, out_sem.at[0])
     store_corr.start()
     receive(SWEEPS, phase)
 
-    deep = lax.broadcasted_iota(jnp.int32, (2 * cz, cz), 0) // 2
-    wide = lax.broadcasted_iota(jnp.int32, (2 * cz, cz), 1)
-    pairing = jnp.where(deep == wide, 0.125, 0.0).astype(jnp.float32)
-
-    def coarse_plane(i, _):
+    wide = lax.broadcasted_iota(jnp.int32, (cy // 4, cz), 1)
+    even = wide % 2 == 0
+    half = cz // 2
+    in_place = jnp.where(wide < half, 2 * wide, 2 * (wide - half) + 1)
+    beside = jnp.where(wide < half, 2 * wide + 1, 2 * (wide - half))
+
+    def pick(v, lanes):
+        return jnp.take_along_axis(v, lanes, axis=1, mode="promise_in_bounds")
+
+    def coarse_plane(i):
         sums = [None] * 4
         for x in (2 * i, 2 * i + 1):
             at = pl.ds(lo, cy)
             mid = phase[x + 1, at, :]
-            half = 0.5 * rhs[1, x]
+            weight = 0.0625 * rhs[1, x]
             before, after = along_depth(mid)
             fields = (
                 mid,
-                half * (phase[x + 2, at, :] - phase[x, at, :]),
-                half * (phase[x + 1, pl.ds(lo + 1, cy), :] - phase[x + 1, pl.ds(lo - 1, cy), :]),
-                half * (after - before),
+                weight * (phase[x + 2, at, :] - phase[x, at, :]),
+                weight * (phase[x + 1, pl.ds(lo + 1, cy), :] - phase[x + 1, pl.ds(lo - 1, cy), :]),
+                weight * (after - before),
             )
             sums = [f if s is None else s + f for s, f in zip(sums, fields)]
-        for f in range(4):
-            slab[f] = sums[f]
-        rows = []
+        sums[0] = 0.125 * sums[0]
         quarter = cy // 4
         for f in range(4):
-            part = [slab[f, pl.ds(k, quarter, stride=4), :] for k in range(4)]
-            rows.append(jnp.concatenate([part[0] + part[1], part[2] + part[3]], axis=1))
-        both = jnp.concatenate(rows, axis=0)
-        mean = jnp.dot(
-            both, pairing, precision=lax.Precision.HIGHEST, preferred_element_type=jnp.float32
-        )
+            slab[lax.rem(i, 4), f] = sums[f]
         for f in range(4):
+            part = [slab[lax.rem(i, 4), f, pl.ds(k, quarter, stride=4), :] for k in range(4)]
+            left, right = part[0] + part[1], part[2] + part[3]
+            mean = pick(jnp.where(even, left, right), in_place)
+            mean = mean + pick(jnp.where(even, right, left), beside)
             for q in range(4):
-                base = f * quarter + q * 4
-                packed[i * 4 + q, f * 4 : f * 4 + 4, :] = mean[base : base + 4, :]
-        return 0
-
-    lax.fori_loop(0, cx // 2, coarse_plane, 0)
+                packed[i * 4 + q, f * 4 : f * 4 + 4, :] = mean[q * 4 : q * 4 + 4, :]
+
+    planes(0, cx // 2, 4, coarse_plane)
 
     def unit_copy(peer):
         return pltpu.make_async_remote_copy(
@@ -294,7 +312,7 @@
             dst_ref=recv.at[pl.ds(me * unit_rows, unit_rows)],
             send_sem=unit_send,
             recv_sem=unit_recv,
-            device_id=(peer // ngy, peer % ngy),
+            device_id=(peer // ngy, lax.rem(peer, ngy)),
             device_id_type=MESH,
         )
 
@@ -368,7 +386,7 @@
             pltpu.VMEM((2,) + padded, f32),
             pltpu.VMEM((2,) + padded, f32),
             pltpu.VMEM(padded, f32),
-            pltpu.VMEM((4, cy, cz), f32),
+            pltpu.VMEM((4, 4, cy, cz), f32),
             pltpu.VMEM((ndev, unit_rows, cz), f32),
             pltpu.VMEM((ndev, unit_rows, cz), f32),
             pltpu.VMEM((ndev * unit_rows, cz), f32),
@@ -383,7 +401,7 @@
             pltpu.SemaphoreType.DMA,
         ],
         compiler_params=pltpu.CompilerParams(
-            has_side_effects=True, vmem_limit_bytes=56 * 1024 * 1024
+            collective_id=0, has_side_effects=True, vmem_limit_bytes=56 * 1024 * 1024
         ),
     )(order, right_side, well_coef, mobility_coef, coupling, phase_old, velocity)
 

time: 92.8 us -> 63.8 us (0.69)
  Pallas kernels: 85 us -> 56 us
    pallas_call x1, Pallas kernels: 85 us -> 56 us  [body(): pl.pallas_call(functools.partial(kernel_body, (ngx, ngy, cx, cy, cz, chun...]
where the time goes in v1:
time: 63.8 us; the launch traced here: 63.7 us
  Pallas kernels  56 us (88%)
  local copies, waits for them, and re-layouts  5.74 us (9%)
  other arithmetic  1.28 us (2%)
  between operations  0.65 us (1%)
    pallas_call x1, Pallas kernels, body(): pl.pallas_call(functools.partial(kernel_body, (ngx, ngy, cx, cy, cz, chun...  56 us
    unnamed x4, local copies, waits for them, and re-layouts  5.74 us
    reduce_sum x1, other arithmetic, body(): jnp.sum(jnp.where(unit_owner[None, :] == ids[:, None], ids[None, :], 0),...  1.28 us

profile of v1, /device:TPU:1, one launch (start us, length us, event | category | flops | bytes accessed | tf_op | source)
XLA Modules:
  0.0 63.7 jit_solution(2935832557351927192)
XLA Ops:
  0.6 1.3 %select_reduce_fusion.order = s32[128]{0:T(128)} fusion(s32[128]{0:T(128)} %param.12), kind=kLoop, calls=%fused_computation | loop fusion | flops 49024 | bytes 1024 | tf_op jit(solution)/shard_map/reduce_sum | solution.py:368
  1.9 56.0 %shard_map.86 = (f32[2,64,64,128]{3,2,1,0:T(8,128)}, f32[3,128,512]{2,1,0:T(8,128)}) custom-call(s32[128]{0:T(128)} %select_reduce_fusion.order, f32[2,64,64,128]{3,2,1,0:T(8,128)} %rhs_hbm.1, f32[64,64,128]{2,1,0:T(8,128)} %well_hbm.1, f32[64,64,128]{2,1,0:T(8,128)} %mob_hbm.1, f32[64,64,128]{2,1,0:T(8,128)} %cpl_hbm.1, f32[64,64,128]{2,1,0:T(8,128)} %pold_hbm.1, ...), custom_call_target="tpu_custom_call" | custom-call | tf_op jit(solution)/shard_map/pallas_call | solution.py:372
  57.9 0.0 copy-start
  57.9 4.9 %copy.11 = f32[2,64,64,128]{3,2,1,0:T(8,128)} copy(f32[2,64,64,128]{3,2,1,0:T(8,128)} %get-tuple-element.4) | data formatting | bytes 8388608
  62.8 0.0 copy-done
  62.8 0.9 %copy.12 = f32[3,128,512]{2,1,0:T(8,128)} copy(f32[3,128,512]{2,1,0:T(8,128)S(1)} %copy-done) | data formatting | bytes 1572864
Async XLA Ops:
  57.9 4.9 %copy-start = (f32[3,128,512]{2,1,0:T(8,128)S(1)}, f32[3,128,512]{2,1,0:T(8,128)}, u32[]{:S(2)}) copy-start(f32[3,128,512]{2,1,0:T(8,128)} %get-tuple-element.5) | copy-start | bytes 2359300

commit v2 on v1

v2 whole, which is shorter than its diff:
```python
import functools

import jax
import jax.numpy as jnp
from jax import lax
from jax.experimental import pallas as pl
from jax.experimental.pallas import tpu as pltpu
from jax.sharding import PartitionSpec as P

SWEEPS = 3
LOW_BOUND = 0.15
HIGH_BOUND = 1.85
THETA = (HIGH_BOUND + LOW_BOUND) / 2.0
DELTA = (HIGH_BOUND - LOW_BOUND) / 2.0
SIGMA = THETA / DELTA

PAD = 8
MESH = pl.DeviceIdType.MESH


def recurrence():
    table, scales = [], [1.0]
    rho = 1.0 / SIGMA
    decay_before, gain_before = 0.0, 0.0
    for sweep in range(SWEEPS):
        rho_new = 1.0 / (2.0 * SIGMA - rho)
        decay, gain = rho_new * rho, 2.0 * rho_new / DELTA
        if sweep == 0:
            table.append(((decay + gain * (THETA - 1.0)) / gain, 0.0))
        else:
            ratio = gain / gain_before
            before = -ratio * decay_before * scales[-2] / (gain * scales[-1])
            table.append(((decay + ratio - gain) / gain, before))
        scales.append(scales[-1] * gain)
        decay_before, gain_before, rho = decay, gain, rho_new
    return table, scales


def kernel_body(
    sizes,
    owner,
    rhs_hbm,
    well_hbm,
    mob_hbm,
    cpl_hbm,
    pold_hbm,
    vel_hbm,
    corr,
    mom,
    owner_row,
    order_row,
    order,
    inv,
    inv_edge,
    cpl,
    pold,
    dir0,
    dir1,
    dir2,
    phase,
    x_recv,
    y_send,
    y_recv,
    slab,
    packed,
    stage,
    recv,
    vel,
    load_sem,
    rest_sem,
    halo_send,
    halo_recv,
    unit_send,
    unit_recv,
):
    ngx, ngy, cx, cy, cz, chunks = sizes
    ndev = ngx * ngy
    gx, gy = lax.axis_index("gx"), lax.axis_index("gy")
    me = gx * ngy + gy
    per = cx // chunks
    pitch = cy + 2 * PAD
    f32 = jnp.float32

    def padded(x, rows=cy):
        return pl.ds(pl.multiple_of((x + 1) * pitch + PAD, 8), rows)

    def shifted(x, by):
        return pl.ds((x + 1) * pitch + PAD + by, cy)

    def plain(x):
        return pl.ds(pl.multiple_of(x * cy, 8), cy)

    def padded_column(y):
        return pl.ds(pitch + PAD + y, cx, stride=pitch)

    def plain_column(y):
        return pl.ds(y, cx, stride=cy)

    ends_x, ends_y = (0, cx - 1), (0, cy - 1)

    def load_chunk(i):
        at = pl.ds(i * per * cy, per * cy)
        return (
            pltpu.make_async_copy(rhs_hbm.at[:, at], corr.at[:, at], load_sem.at[i, 0]),
            pltpu.make_async_copy(well_hbm.at[at], inv.at[0, at], load_sem.at[i, 1]),
            pltpu.make_async_copy(mob_hbm.at[at], inv.at[1, at], load_sem.at[i, 2]),
        )

    load_cpl = pltpu.make_async_copy(cpl_hbm, cpl, rest_sem.at[0])
    load_pold = pltpu.make_async_copy(pold_hbm, pold, rest_sem.at[1])
    load_vel = pltpu.make_async_copy(vel_hbm, vel, rest_sem.at[2])
    load_owner = pltpu.make_async_copy(owner, owner_row, rest_sem.at[4])
    load_owner.start()
    chunk_order = [0, chunks - 1] + list(range(1, chunks - 1))
    for i in chunk_order:
        for copy in load_chunk(i):
            copy.start()
    load_cpl.start()
    load_pold.start()
    load_vel.start()

    barrier = pltpu.get_barrier_semaphore()

    def greet(k, _):
        peer = lax.rem(me + k, ndev)
        pl.semaphore_signal(
            barrier, inc=1, device_id=(peer // ngy, lax.rem(peer, ngy)), device_id_type=MESH
        )
        return 0

    lax.fori_loop(1, ndev, greet, 0)

    down = lax.broadcasted_iota(jnp.int32, (ndev, ndev), 0)
    across = lax.broadcasted_iota(jnp.int32, (ndev, ndev), 1)
    load_owner.wait()
    unit_of = jnp.max(jnp.where(owner_row[...] == down, across, 0), axis=1, keepdims=True)
    order_row[...] = jnp.max(jnp.where(down == across, unit_of, 0), axis=0, keepdims=True)
    save_order = pltpu.make_async_copy(order_row, order, rest_sem.at[3])
    save_order.start()

    for buf in (dir0, dir1, dir2):
        for c in range(2):
            for x in (-1, cx):
                buf[c, padded(x), :] = jnp.zeros((cy, cz), f32)
            for y in (-1, cy):
                buf[c, padded_column(y), :] = jnp.zeros((cx, cz), f32)
    for y in (-1, cy):
        phase[padded_column(y), :] = jnp.zeros((cx, cz), f32)

    @pl.when(gx == 0)
    def _():
        phase[padded(-1), :] = jnp.zeros((cy, cz), f32)

    @pl.when(gx == ngx - 1)
    def _():
        phase[padded(cx), :] = jnp.zeros((cy, cz), f32)

    targets = ((gx - 1, gy), (gx + 1, gy), (gx, gy - 1), (gx, gy + 1))
    sends = (gx > 0, gx < ngx - 1, gy > 0, gy < ngy - 1)

    def halo_copy(step, way):
        side, other = way % 2, 1 - way % 2
        if way >= 2:
            src, dst = y_send.at[step, side], y_recv.at[step, other]
            if step == SWEEPS:
                src, dst = src.at[0], dst.at[0]
        elif step == SWEEPS:
            src, dst = phase.at[padded(ends_x[side])], phase.at[padded((-1, cx)[other])]
        else:
            src = (dir0, dir1, dir2)[step].at[:, padded(ends_x[side])]
            dst = x_recv.at[step, other]
        return pltpu.make_async_remote_copy(
            src_ref=src,
            dst_ref=dst,
            send_sem=halo_send.at[step, way],
            recv_sem=halo_recv.at[step, way],
            device_id=targets[way],
            device_id_type=MESH,
        )

    def send(step, ways):
        for way in ways:

            @pl.when(sends[way])
            def _(way=way):
                halo_copy(step, way).start()

    def receive(step, way, work):
        @pl.when(sends[way ^ 1])
        def _():
            halo_copy(step, way).wait_recv()
            work()

    def finish(step):
        for way in range(4):

            @pl.when(sends[way])
            def _(way=way):
                halo_copy(step, way).wait_send()

    lane = lax.broadcasted_iota(jnp.int32, (1, cz), 1)
    first_lane, last_lane = lane == 0, lane == cz - 1

    def along_depth(v):
        before = jnp.where(first_lane, 0.0, pltpu.roll(v, 1, axis=1))
        after = jnp.where(last_lane, 0.0, pltpu.roll(v, cz - 1, axis=1))
        return before, after

    def planes(first, last, together, work):
        def some(i, _):
            for k in range(together):
                work(first + i * together + k)
            return 0

        lax.fori_loop(0, (last - first) // together, some, 0)

    def start_plane(x):
        for c in range(2):
            part = 1.0 / (inv[c, plain(x), :] + 6.0)
            inv[c, plain(x), :] = part
            dir0[c, padded(x), :] = part * corr[c, plain(x), :] * (1.0 / THETA)

    for n, i in enumerate(chunk_order):
        for copy in load_chunk(i):
            copy.wait()
        planes(i * per, (i + 1) * per, 4, start_plane)
        if n == 4:
            pl.semaphore_wait(barrier, ndev - 1)
            send(0, (0, 1))
    for side in range(2):
        for c in range(2):
            y_send[0, side, c] = dir0[c, padded_column(ends_y[side]), :]
    send(0, (2, 3))
    for side in range(2):
        for c in range(2):
            inv_edge[side, c] = inv[c, plain_column(ends_y[side]), :]
    load_cpl.wait()

    table, scales = recurrence()

    def own(x, y, rows):
        return pl.ds(pl.multiple_of((x + 1) * pitch + PAD + y, 8), rows)

    def sweep_plane(sweep, x, y, rows):
        now = (dir0, dir1, dir2)[sweep]
        of_now, of_before = table[sweep]
        mid = [now[c, own(x, y, rows), :] for c in range(2)]
        mix = cpl[pl.ds(pl.multiple_of(x * cy + y, 8), rows), :]
        for c in range(2):
            before, after = along_depth(mid[c])
            nbrs = now[c, own(x - 1, y, rows), :] + now[c, own(x + 1, y, rows), :]
            nbrs = nbrs + (now[c, pl.ds((x + 1) * pitch + PAD + y - 1, rows), :] + now[c, pl.ds((x + 1) * pitch + PAD + y + 1, rows), :])
            nbrs = nbrs + (before + after)
            new = of_now * mid[c] + inv[c, pl.ds(pl.multiple_of(x * cy + y, 8), rows), :] * (nbrs - mix * mid[1 - c])
            if sweep > 0:
                new = new + of_before * (dir0, dir1)[sweep - 1][c, own(x, y, rows), :]
            if sweep < SWEEPS - 1:
                (dir1, dir2)[sweep][c, own(x, y, rows), :] = new
            else:
                total = scales[0] * dir0[c, own(x, y, rows), :] + scales[1] * dir1[c, own(x, y, rows), :]
                total = total + (scales[2] * mid[c] + scales[3] * new)
                corr[c, pl.ds(pl.multiple_of(x * cy + y, 8), rows), :] = total
                if c == 0:
                    phase[own(x, y, rows), :] = pold[pl.ds(pl.multiple_of(x * cy + y, 8), rows), :] + total

    def add_halos(sweep):
        last = sweep == SWEEPS - 1
        into = None if last else (dir1, dir2)[sweep]
        for side in range(2):

            def along_x(side=side):
                x = ends_x[side]
                for c in range(2):
                    more = inv[c, plain(x), :] * x_recv[sweep, side, c]
                    if last:
                        corr[c, plain(x), :] += scales[3] * more
                        if c == 0:
                            phase[padded(x), :] += scales[3] * more
                    else:
                        into[c, padded(x), :] += more

            receive(sweep, 1 - side, along_x)
        for side in range(2):

            def along_y(side=side):
                y = ends_y[side]
                for c in range(2):
                    more = inv_edge[side, c] * y_recv[sweep, side, c]
                    if last:
                        corr[c, plain_column(y), :] += scales[3] * more
                        if c == 0:
                            phase[padded_column(y), :] += scales[3] * more
                    else:
                        into[c, padded_column(y), :] += more

            receive(sweep, 3 - side, along_y)
        send(sweep + 1, (0, 1))
        for side in range(2):
            if last:
                y_send[sweep + 1, side, 0] = phase[padded_column(ends_y[side]), :]
            else:
                for c in range(2):
                    y_send[sweep + 1, side, c] = into[c, padded_column(ends_y[side]), :]
        send(sweep + 1, (2, 3))

    for sweep in range(SWEEPS):
        if sweep == SWEEPS - 1:
            load_pold.wait()
        def plane(x, sweep=sweep):
            for y in range(0, cy, 32):
                sweep_plane(sweep, x, y, 32)

        planes(0, cx, 4, plane)
        add_halos(sweep)

    wide = lax.broadcasted_iota(jnp.int32, (cy // 4, cz), 1)
    even = wide % 2 == 0
    half = cz // 2
    in_place = jnp.where(wide < half, 2 * wide, 2 * (wide - half) + 1)
    beside = jnp.where(wide < half, 2 * wide + 1, 2 * (wide - half))

    def pick(v, lanes):
        return jnp.take_along_axis(v, lanes, axis=1, mode="promise_in_bounds")

    def coarse_plane(part, i):
        sums = [None] * 2
        for x in (2 * i, 2 * i + 1):
            weight = 0.0625 * corr[1, plain(x), :]
            if part == 0:
                mid = phase[padded(x), :]
                before, after = along_depth(mid)
                fields = (0.125 * mid, weight * (after - before))
            else:
                fields = (
                    weight * (phase[padded(x + 1), :] - phase[padded(x - 1), :]),
                    weight * (phase[shifted(x, 1), :] - phase[shifted(x, -1), :]),
                )
            sums = [f if s is None else s + f for s, f in zip(sums, fields)]
        quarter = cy // 4
        slot = lax.rem(i, 4)
        for f in range(2):
            slab[slot, f] = sums[f]
        for f in range(2):
            rows = [slab[slot, f, pl.ds(k, quarter, stride=4), :] for k in range(4)]
            left, right = rows[0] + rows[1], rows[2] + rows[3]
            mean = pick(jnp.where(even, left, right), in_place)
            mean = mean + pick(jnp.where(even, right, left), beside)
            for q in range(4):
                packed[part, i * 4 + q, f * 4 : f * 4 + 4, :] = mean[q * 4 : q * 4 + 4, :]

    unit_rows = packed.shape[2]

    def unit_copy(part, peer):
        return pltpu.make_async_remote_copy(
            src_ref=stage.at[part, peer],
            dst_ref=recv.at[part, pl.ds(me * unit_rows, unit_rows)],
            send_sem=unit_send.at[part],
            recv_sem=unit_recv.at[part],
            device_id=(peer // ngy, lax.rem(peer, ngy)),
            device_id_type=MESH,
        )

    def ship(part):
        def one(k):
            peer = lax.rem(me + k, ndev)
            stage[part, peer] = packed[part, order[0, peer]]
            unit_copy(part, peer).start()

        planes(1, ndev - 1, 6, one)
        one(ndev - 1)
        recv[part, pl.ds(me * unit_rows, unit_rows), :] = packed[part, order[0, me]]

    def arrive(part):
        others = recv.at[part, pl.ds(0, (ndev - 1) * unit_rows)]
        pltpu.make_async_copy(others, others, unit_recv.at[part]).wait()

    save_order.wait()
    planes(0, cx // 2, 4, functools.partial(coarse_plane, 0))
    ship(0)
    for way in range(2):
        receive(SWEEPS, way, lambda: None)
    for side in range(2):

        def beyond(side=side):
            phase[padded_column((-1, cy)[side]), :] = y_recv[SWEEPS, side, 0]

        receive(SWEEPS, 3 - side, beyond)
    planes(0, cx // 2, 4, functools.partial(coarse_plane, 1))
    ship(1)

    for step in range(SWEEPS + 1):
        finish(step)
    load_vel.wait()

    place = lax.rem(lane, cz // 2)
    bottom, top = place == 0, place == cz // 2 - 1

    def product(v, density, visc, weight):
        below = jnp.where(bottom, 0.0, pltpu.roll(v, 1, axis=1))
        flux = weight * (v - below)
        above = jnp.where(top, -visc * v, pltpu.roll(flux, cz - 1, axis=1))
        return density * v - (above - flux)

    def get(part, f, r):
        return recv[part, pl.ds(f * 4 + r, ndev, stride=unit_rows), :]

    def factors(r):
        mean = get(0, 0, r)
        density = 0.1 + 0.45 * (1.0 + mean)
        visc = 0.2 + 0.4 * (1.0 + mean)
        weight = 0.5 * (visc + jnp.where(bottom, visc, pltpu.roll(visc, 1, axis=1)))
        return density, visc, weight

    arrive(0)
    for r in range(4):
        at = pl.ds(r * cz, cz)
        parts = factors(r)
        for c in range(3):
            stress = product(vel[c, :, at], *parts)
            mom[c, :, at] = product(stress - get(0, 1, r), *parts) if c == 2 else stress
    arrive(1)
    for r in range(4):
        at = pl.ds(r * cz, cz)
        parts = factors(r)
        for c in range(2):
            mom[c, :, at] = product(mom[c, :, at] - get(1, c, r), *parts)

    for part in range(2):
        sent = stage.at[part, pl.ds(0, ndev - 1)]
        pltpu.make_async_copy(sent, sent, unit_send.at[part]).wait()


def body(ngx, ngy, right_side, well_coef, mobility_coef, coupling, phase_old, unit_owner, velocity):
    _, cx, cy, cz = right_side.shape
    ndev = ngx * ngy
    chunks = 8
    unit_rows = 2 * (velocity.shape[2] // cz)
    flat = cx * cy
    padded = (cx + 2) * (cy + 2 * PAD)
    hbm_spec = pl.BlockSpec(memory_space=pltpu.HBM)
    vmem_spec = pl.BlockSpec(memory_space=pltpu.VMEM)
    f32 = jnp.float32
    steps = SWEEPS + 1
    hbm = lambda x: pltpu.with_memory_space_constraint(x, pltpu.HBM)
    correction, momentum = pl.pallas_call(
        functools.partial(kernel_body, (ngx, ngy, cx, cy, cz, chunks)),
        out_shape=(
            pltpu.VMEM((2, flat, cz), f32),
            pltpu.VMEM(velocity.shape, f32),
        ),
        in_specs=[hbm_spec] * 7,
        out_specs=(vmem_spec, vmem_spec),
        scratch_shapes=[
            pltpu.VMEM((1, ndev), jnp.int32),
            pltpu.VMEM((1, ndev), jnp.int32),
            pltpu.SMEM((1, ndev), jnp.int32),
            pltpu.VMEM((2, flat, cz), f32),
            pltpu.VMEM((2, 2, cx, cz), f32),
            pltpu.VMEM((flat, cz), f32),
            pltpu.VMEM((flat, cz), f32),
            pltpu.VMEM((2, padded, cz), f32),
            pltpu.VMEM((2, padded, cz), f32),
            pltpu.VMEM((2, padded, cz), f32),
            pltpu.VMEM((padded, cz), f32),
            pltpu.VMEM((SWEEPS, 2, 2, cy, cz), f32),
            pltpu.VMEM((steps, 2, 2, cx, cz), f32),
            pltpu.VMEM((steps, 2, 2, cx, cz), f32),
            pltpu.VMEM((4, 2, cy, cz), f32),
            pltpu.VMEM((2, ndev, unit_rows, cz), f32),
            pltpu.VMEM((2, ndev, unit_rows, cz), f32),
            pltpu.VMEM((2, ndev * unit_rows, cz), f32),
            pltpu.VMEM(velocity.shape, f32),
            pltpu.SemaphoreType.DMA((chunks, 3)),
            pltpu.SemaphoreType.DMA((5,)),
            pltpu.SemaphoreType.DMA((steps, 4)),
            pltpu.SemaphoreType.DMA((steps, 4)),
            pltpu.SemaphoreType.DMA((2,)),
            pltpu.SemaphoreType.DMA((2,)),
        ],
        compiler_params=pltpu.CompilerParams(
            collective_id=0, has_side_effects=True, vmem_limit_bytes=48 * 1024 * 1024
        ),
    )(
        hbm(unit_owner.reshape(1, ndev)),
        hbm(right_side.reshape(2, flat, cz)),
        hbm(well_coef.reshape(flat, cz)),
        hbm(mobility_coef.reshape(flat, cz)),
        hbm(coupling.reshape(flat, cz)),
        hbm(phase_old.reshape(flat, cz)),
        hbm(velocity),
    )
    return correction.reshape(right_side.shape), momentum


def solution(mesh):
    return jax.shard_map(
        functools.partial(body, mesh.shape["gx"], mesh.shape["gy"]),
        mesh=mesh,
        in_specs=(
            P(None, "gx", "gy", None),
            P("gx", "gy", None),
            P("gx", "gy", None),
            P("gx", "gy", None),
            P("gx", "gy", None),
            P(("gx", "gy")),
            P(None, ("gx", "gy"), None),
        ),
        out_specs=(P(None, "gx", "gy", None), P(None, ("gx", "gy"), None)),
        check_vma=False,
    )
```

time: 63.8 us -> 50.7 us (0.79)
  Pallas kernels: 56 us -> 47.1 us
  local copies, waits for them, and re-layouts: 5.74 us -> 2.89 us
  other arithmetic: 1.28 us -> 0 us
    pallas_call x1, Pallas kernels: 56 us -> 47.1 us  [body(): pl.pallas_call(functools.partial(kernel_body, (ngx, ngy, cx, cy, cz, chun...]
    unnamed x4 -> x2, local copies, waits for them, and re-layouts: 5.74 us -> 2.89 us
    reduce_sum x1 -> x0, other arithmetic: 1.28 us -> none  [body(): jnp.sum(jnp.where(unit_owner[None, :] == ids[:, None], ids[None, :], 0),...]
where the time goes in v2:
time: 50.7 us; the launch traced here: 50.6 us
  Pallas kernels  47.1 us (93%)
  local copies, waits for them, and re-layouts  2.89 us (6%)
  between operations  0.64 us (1%)
    pallas_call x1, Pallas kernels, body(): pl.pallas_call(functools.partial(kernel_body, (ngx, ngy, cx, cy, cz, chun...  47.1 us
    unnamed x2, local copies, waits for them, and re-layouts  2.89 us

profile of v2, /device:TPU:1, one launch (start us, length us, event | category | flops | bytes accessed | tf_op | source)
XLA Modules:
  0.0 50.6 jit_solution(1453732039070214471)
XLA Ops:
  0.6 47.1 %shard_map.86 = (f32[2,4096,128]{2,1,0:T(8,128)S(1)}, f32[3,128,512]{2,1,0:T(8,128)S(1)}) custom-call(s32[1,128]{1,0:T(1,128)} %bitcast.13, f32[2,4096,128]{2,1,0:T(8,128)} %bitcast.8, f32[4096,128]{1,0:T(8,128)} %bitcast.9, f32[4096,128]{1,0:T(8,128)} %bitcast.10, f32[4096,128]{1,0:T(8,128)} %bitcast.11, f32[4096,128]{1,0:T(8,128)} %bitcast.12, ...), custom_call_target="tpu_custom_call" | custom-call | tf_op jit(solution)/shard_map/pallas_call | solution.py:445
  47.7 2.0 %copy.11 = f32[2,64,64,128]{3,2,1,0:T(8,128)} copy(f32[2,64,64,128]{3,2,1,0:T(8,128)S(1)} %bitcast.7) | data formatting | bytes 8388608
  49.8 0.9 %copy.12 = f32[3,128,512]{2,1,0:T(8,128)} copy(f32[3,128,512]{2,1,0:T(8,128)S(1)} %get-tuple-element.7) | data formatting | bytes 1572864

commit v3 on v2

--- a/solution.py
+++ b/solution.py
@@ -15,7 +15,9 @@
 SIGMA = THETA / DELTA
 
 PAD = 8
+OUT_PIECES = 4
 MESH = pl.DeviceIdType.MESH
+FLAT = pl.DeviceIdType.LOGICAL
 
 
 def recurrence():
@@ -36,6 +38,32 @@
     return table, scales
 
 
+def column_products(cz, recv):
+    unit_rows = 8
+    units = recv.shape[1] // unit_rows
+    lane = lax.broadcasted_iota(jnp.int32, (1, cz), 1)
+    place = lax.rem(lane, cz // 2)
+    bottom, top = place == 0, place == cz // 2 - 1
+
+    def product(v, density, visc, weight):
+        below = jnp.where(bottom, 0.0, pltpu.roll(v, 1, axis=1))
+        flux = weight * (v - below)
+        above = jnp.where(top, -visc * v, pltpu.roll(flux, cz - 1, axis=1))
+        return density * v - (above - flux)
+
+    def get(part, f, r):
+        return recv[part, pl.ds(f * 4 + r, units, stride=unit_rows), :]
+
+    def factors(r):
+        mean = get(0, 0, r)
+        density = 0.1 + 0.45 * (1.0 + mean)
+        visc = 0.2 + 0.4 * (1.0 + mean)
+        weight = 0.5 * (visc + jnp.where(bottom, visc, pltpu.roll(visc, 1, axis=1)))
+        return density, visc, weight
+
+    return product, get, factors
+
+
 def kernel_body(
     sizes,
     owner,
@@ -45,12 +73,17 @@
     cpl_hbm,
     pold_hbm,
     vel_hbm,
+    rhs_rows,
+    well_rows,
+    mob_rows,
     corr,
     mom,
+    recv,
     owner_row,
     order_row,
     order,
     inv,
+    rhs_edge,
     inv_edge,
     cpl,
     pold,
@@ -64,9 +97,9 @@
     slab,
     packed,
     stage,
-    recv,
     vel,
     load_sem,
+    edge_sem,
     rest_sem,
     halo_send,
     halo_recv,
@@ -81,6 +114,14 @@
     pitch = cy + 2 * PAD
     f32 = jnp.float32
 
+    def planes(first, last, together, work):
+        def some(i, _):
+            for k in range(together):
+                work(first + i * together + k)
+            return 0
+
+        lax.fori_loop(0, (last - first) // together, some, 0)
+
     def padded(x, rows=cy):
         return pl.ds(pl.multiple_of((x + 1) * pitch + PAD, 8), rows)
 
@@ -97,6 +138,16 @@
         return pl.ds(y, cx, stride=cy)
 
     ends_x, ends_y = (0, cx - 1), (0, cy - 1)
+
+    barrier = pltpu.get_barrier_semaphore()
+
+    def greet(k):
+        pl.semaphore_signal(
+            barrier, inc=1, device_id=lax.rem(me + k, ndev), device_id_type=FLAT
+        )
+
+    planes(1, ndev - 1, 9, greet)
+    greet(ndev - 1)
 
     def load_chunk(i):
         at = pl.ds(i * per * cy, per * cy)
@@ -106,29 +157,29 @@
             pltpu.make_async_copy(mob_hbm.at[at], inv.at[1, at], load_sem.at[i, 2]),
         )
 
+    def load_edge(side):
+        y = ends_y[side]
+        return (
+            pltpu.make_async_copy(rhs_rows.at[:, :, y], rhs_edge.at[side], edge_sem.at[side, 0]),
+            pltpu.make_async_copy(well_rows.at[:, y], inv_edge.at[side, 0], edge_sem.at[side, 1]),
+            pltpu.make_async_copy(mob_rows.at[:, y], inv_edge.at[side, 1], edge_sem.at[side, 2]),
+        )
+
     load_cpl = pltpu.make_async_copy(cpl_hbm, cpl, rest_sem.at[0])
     load_pold = pltpu.make_async_copy(pold_hbm, pold, rest_sem.at[1])
     load_vel = pltpu.make_async_copy(vel_hbm, vel, rest_sem.at[2])
     load_owner = pltpu.make_async_copy(owner, owner_row, rest_sem.at[4])
     load_owner.start()
     chunk_order = [0, chunks - 1] + list(range(1, chunks - 1))
+    for side in range(2):
+        for copy in load_edge(side):
+            copy.start()
     for i in chunk_order:
         for copy in load_chunk(i):
             copy.start()
     load_cpl.start()
     load_pold.start()
     load_vel.start()
-
-    barrier = pltpu.get_barrier_semaphore()
-
-    def greet(k, _):
-        peer = lax.rem(me + k, ndev)
-        pl.semaphore_signal(
-            barrier, inc=1, device_id=(peer // ngy, lax.rem(peer, ngy)), device_id_type=MESH
-        )
-        return 0
-
-    lax.fori_loop(1, ndev, greet, 0)
 
     down = lax.broadcasted_iota(jnp.int32, (ndev, ndev), 0)
     across = lax.broadcasted_iota(jnp.int32, (ndev, ndev), 1)
@@ -206,34 +257,26 @@
         after = jnp.where(last_lane, 0.0, pltpu.roll(v, cz - 1, axis=1))
         return before, after
 
-    def planes(first, last, together, work):
-        def some(i, _):
-            for k in range(together):
-                work(first + i * together + k)
-            return 0
-
-        lax.fori_loop(0, (last - first) // together, some, 0)
-
     def start_plane(x):
         for c in range(2):
             part = 1.0 / (inv[c, plain(x), :] + 6.0)
             inv[c, plain(x), :] = part
             dir0[c, padded(x), :] = part * corr[c, plain(x), :] * (1.0 / THETA)
 
+    for side in range(2):
+        for copy in load_edge(side):
+            copy.wait()
+        for c in range(2):
+            part = 1.0 / (inv_edge[side, c] + 6.0)
+            inv_edge[side, c] = part
+            y_send[0, side, c] = part * rhs_edge[side, c] * (1.0 / THETA)
     for n, i in enumerate(chunk_order):
         for copy in load_chunk(i):
             copy.wait()
         planes(i * per, (i + 1) * per, 4, start_plane)
-        if n == 4:
+        if n == 1:
             pl.semaphore_wait(barrier, ndev - 1)
-            send(0, (0, 1))
-    for side in range(2):
-        for c in range(2):
-            y_send[0, side, c] = dir0[c, padded_column(ends_y[side]), :]
-    send(0, (2, 3))
-    for side in range(2):
-        for c in range(2):
-            inv_edge[side, c] = inv[c, plain_column(ends_y[side]), :]
+            send(0, (0, 1, 2, 3))
     load_cpl.wait()
 
     table, scales = recurrence()
@@ -356,8 +399,8 @@
             dst_ref=recv.at[part, pl.ds(me * unit_rows, unit_rows)],
             send_sem=unit_send.at[part],
             recv_sem=unit_recv.at[part],
-            device_id=(peer // ngy, lax.rem(peer, ngy)),
-            device_id_type=MESH,
+            device_id=peer,
+            device_id_type=FLAT,
         )
 
     def ship(part):
@@ -392,25 +435,7 @@
         finish(step)
     load_vel.wait()
 
-    place = lax.rem(lane, cz // 2)
-    bottom, top = place == 0, place == cz // 2 - 1
-
-    def product(v, density, visc, weight):
-        below = jnp.where(bottom, 0.0, pltpu.roll(v, 1, axis=1))
-        flux = weight * (v - below)
-        above = jnp.where(top, -visc * v, pltpu.roll(flux, cz - 1, axis=1))
-        return density * v - (above - flux)
-
-    def get(part, f, r):
-        return recv[part, pl.ds(f * 4 + r, ndev, stride=unit_rows), :]
-
-    def factors(r):
-        mean = get(0, 0, r)
-        density = 0.1 + 0.45 * (1.0 + mean)
-        visc = 0.2 + 0.4 * (1.0 + mean)
-        weight = 0.5 * (visc + jnp.where(bottom, visc, pltpu.roll(visc, 1, axis=1)))
-        return density, visc, weight
-
+    product, get, factors = column_products(cz, recv)
     arrive(0)
     for r in range(4):
         at = pl.ds(r * cz, cz)
@@ -419,15 +444,32 @@
             stress = product(vel[c, :, at], *parts)
             mom[c, :, at] = product(stress - get(0, 1, r), *parts) if c == 2 else stress
     arrive(1)
+
+    for part in range(2):
+        sent = stage.at[part, pl.ds(0, ndev - 1)]
+        pltpu.make_async_copy(sent, sent, unit_send.at[part]).wait()
+
+
+def output_body(cz, corr, mom, recv, corr_hbm, mom_hbm, rest, sem):
+    size = corr.shape[1] * 2 // OUT_PIECES
+    copies = []
+    for i in range(OUT_PIECES):
+        c, at = i % 2, pl.ds(i // 2 * size, size)
+        copies.append(pltpu.make_async_copy(corr.at[c, at], corr_hbm.at[c, at], sem.at[i]))
+    copies.append(pltpu.make_async_copy(mom.at[2], mom_hbm.at[2], sem.at[OUT_PIECES]))
+    for copy in copies:
+        copy.start()
+    product, get, factors = column_products(cz, recv)
     for r in range(4):
         at = pl.ds(r * cz, cz)
         parts = factors(r)
         for c in range(2):
-            mom[c, :, at] = product(mom[c, :, at] - get(1, c, r), *parts)
-
-    for part in range(2):
-        sent = stage.at[part, pl.ds(0, ndev - 1)]
-        pltpu.make_async_copy(sent, sent, unit_send.at[part]).wait()
+            rest[c, :, at] = product(mom[c, :, at] - get(1, c, r), *parts)
+    store = pltpu.make_async_copy(rest, mom_hbm.at[pl.ds(0, 2)], sem.at[OUT_PIECES + 1])
+    store.start()
+    for copy in copies:
+        copy.wait()
+    store.wait()
 
 
 def body(ngx, ngy, right_side, well_coef, mobility_coef, coupling, phase_old, unit_owner, velocity):
@@ -442,19 +484,21 @@
     f32 = jnp.float32
     steps = SWEEPS + 1
     hbm = lambda x: pltpu.with_memory_space_constraint(x, pltpu.HBM)
-    correction, momentum = pl.pallas_call(
+    parts = pl.pallas_call(
         functools.partial(kernel_body, (ngx, ngy, cx, cy, cz, chunks)),
         out_shape=(
             pltpu.VMEM((2, flat, cz), f32),
             pltpu.VMEM(velocity.shape, f32),
+            pltpu.VMEM((2, ndev * unit_rows, cz), f32),
         ),
-        in_specs=[hbm_spec] * 7,
-        out_specs=(vmem_spec, vmem_spec),
+        in_specs=[hbm_spec] * 10,
+        out_specs=(vmem_spec,) * 3,
         scratch_shapes=[
             pltpu.VMEM((1, ndev), jnp.int32),
             pltpu.VMEM((1, ndev), jnp.int32),
             pltpu.SMEM((1, ndev), jnp.int32),
             pltpu.VMEM((2, flat, cz), f32),
+            pltpu.VMEM((2, 2, cx, cz), f32),
             pltpu.VMEM((2, 2, cx, cz), f32),
             pltpu.VMEM((flat, cz), f32),
             pltpu.VMEM((flat, cz), f32),
@@ -468,9 +512,9 @@
             pltpu.VMEM((4, 2, cy, cz), f32),
             pltpu.VMEM((2, ndev, unit_rows, cz), f32),
             pltpu.VMEM((2, ndev, unit_rows, cz), f32),
-            pltpu.VMEM((2, ndev * unit_rows, cz), f32),
             pltpu.VMEM(velocity.shape, f32),
             pltpu.SemaphoreType.DMA((chunks, 3)),
+            pltpu.SemaphoreType.DMA((2, 3)),
             pltpu.SemaphoreType.DMA((5,)),
             pltpu.SemaphoreType.DMA((steps, 4)),
             pltpu.SemaphoreType.DMA((steps, 4)),
@@ -488,7 +532,25 @@
         hbm(coupling.reshape(flat, cz)),
         hbm(phase_old.reshape(flat, cz)),
         hbm(velocity),
+        hbm(right_side),
+        hbm(well_coef),
+        hbm(mobility_coef),
     )
+    vmem = lambda x: pltpu.with_memory_space_constraint(x, pltpu.VMEM)
+    correction, momentum = pl.pallas_call(
+        functools.partial(output_body, cz),
+        out_shape=(
+            jax.ShapeDtypeStruct((2, flat, cz), f32),
+            jax.ShapeDtypeStruct(velocity.shape, f32),
+        ),
+        in_specs=[vmem_spec] * 3,
+        out_specs=(hbm_spec, hbm_spec),
+        scratch_shapes=[
+            pltpu.VMEM((2,) + velocity.shape[1:], f32),
+            pltpu.SemaphoreType.DMA((OUT_PIECES + 2,)),
+        ],
+        compiler_params=pltpu.CompilerParams(vmem_limit_bytes=8 * 1024 * 1024),
+    )(*[vmem(x) for x in parts])
     return correction.reshape(right_side.shape), momentum
 
 

time: 50.7 us -> 49 us (0.966)
  local copies, waits for them, and re-layouts: 2.89 us -> 0 us
  Pallas kernels: 47.1 us -> 48.3 us
    unnamed x2 -> x0, local copies, waits for them, and re-layouts: 2.89 us -> none
    pallas_call x0 -> x1, Pallas kernels: none -> 2.31 us  [body(): pl.pallas_call(functools.partial(output_body, cz), out_shape=(jax.ShapeDt...]
    pallas_call x1, Pallas kernels: 47.1 us -> 46 us  [body(): pl.pallas_call(functools.partial(kernel_body, (ngx, ngy, cx, cy, cz, chun...]
where the time goes in v3:
time: 49 us; the launch traced here: 48.9 us
  Pallas kernels  48.3 us (99%)
  between operations  0.64 us (1%)
    pallas_call x1, Pallas kernels, body(): pl.pallas_call(functools.partial(kernel_body, (ngx, ngy, cx, cy, cz, chun...  46 us
    pallas_call x1, Pallas kernels, body(): pl.pallas_call(functools.partial(output_body, cz), out_shape=(jax.ShapeDt...  2.31 us

profile of v3, /device:TPU:1, one launch (start us, length us, event | category | flops | bytes accessed | tf_op | source)
XLA Modules:
  0.0 48.9 jit_solution(7092989565114627830)
XLA Ops:
  0.6 46.0 %shard_map.86 = (f32[2,4096,128]{2,1,0:T(8,128)S(1)}, f32[3,128,512]{2,1,0:T(8,128)S(1)}, f32[2,1024,128]{2,1,0:T(8,128)S(1)}) custom-call(s32[1,128]{1,0:T(1,128)} %bitcast.12, f32[2,4096,128]{2,1,0:T(8,128)} %bitcast.7, f32[4096,128]{1,0:T(8,128)} %bitcast.8, f32[4096,128]{1,0:T(8,128)} %bitcast.9, f32[4096,128]{1,0:T(8,128)} %bitcast.10, ...), custom_call_target="tpu_custom_call" | custom-call | tf_op jit(solution)/shard_map/pallas_call | solution.py:487
  46.6 2.3 %shard_map.87 = (f32[2,4096,128]{2,1,0:T(8,128)}, f32[3,128,512]{2,1,0:T(8,128)}) custom-call(f32[2,4096,128]{2,1,0:T(8,128)S(1)} %get-tuple-element.7.corr, f32[3,128,512]{2,1,0:T(8,128)S(1)} %get-tuple-element.8.mom, f32[2,1024,128]{2,1,0:T(8,128)S(1)} %get-tuple-element.9.recv), custom_call_target="tpu_custom_call" | custom-call | tf_op jit(solution)/shard_map/pallas_call | solution.py:540

commit v4 on v3

--- a/solution.py
+++ b/solution.py
@@ -146,7 +146,7 @@
             barrier, inc=1, device_id=lax.rem(me + k, ndev), device_id_type=FLAT
         )
 
-    planes(1, ndev - 1, 9, greet)
+    planes(1, ndev - 1, 21, greet)
     greet(ndev - 1)
 
     def load_chunk(i):
@@ -346,16 +346,6 @@
                     y_send[sweep + 1, side, c] = into[c, padded_column(ends_y[side]), :]
         send(sweep + 1, (2, 3))
 
-    for sweep in range(SWEEPS):
-        if sweep == SWEEPS - 1:
-            load_pold.wait()
-        def plane(x, sweep=sweep):
-            for y in range(0, cy, 32):
-                sweep_plane(sweep, x, y, 32)
-
-        planes(0, cx, 4, plane)
-        add_halos(sweep)
-
     wide = lax.broadcasted_iota(jnp.int32, (cy // 4, cz), 1)
     even = wide % 2 == 0
     half = cz // 2
@@ -364,6 +354,28 @@
 
     def pick(v, lanes):
         return jnp.take_along_axis(v, lanes, axis=1, mode="promise_in_bounds")
+
+    def coarse_outer(i):
+        sums = [None] * 2
+        for x in (2 * i, 2 * i + 1):
+            outer = lambda ref, at: jnp.concatenate(
+                [ref[pl.ds(at, 8), :], ref[pl.ds(at + cy - 8, 8), :]], axis=0
+            )
+            mid = outer(phase, pl.multiple_of((x + 1) * pitch + PAD, 8))
+            before, after = along_depth(mid)
+            weight = 0.0625 * outer(corr.at[1], pl.multiple_of(x * cy, 8))
+            fields = (0.125 * mid, weight * (after - before))
+            sums = [f if s is None else s + f for s, f in zip(sums, fields)]
+        slot = lax.rem(i, 4)
+        for f in range(2):
+            slab[slot, f, 0:16] = sums[f]
+        for f in range(2):
+            rows = [slab[slot, f, pl.ds(k, 4, stride=4), :] for k in range(4)]
+            left, right = rows[0] + rows[1], rows[2] + rows[3]
+            mean = pick(jnp.where(even[0:4], left, right), in_place[0:4])
+            mean = mean + pick(jnp.where(even[0:4], right, left), beside[0:4])
+            packed[0, i * 4, f * 4 : f * 4 + 2, :] = mean[0:2, :]
+            packed[0, i * 4 + 3, f * 4 + 2 : f * 4 + 4, :] = mean[2:4, :]
 
     def coarse_plane(part, i):
         sums = [None] * 2
@@ -391,6 +403,18 @@
             for q in range(4):
                 packed[part, i * 4 + q, f * 4 : f * 4 + 4, :] = mean[q * 4 : q * 4 + 4, :]
 
+    for sweep in range(SWEEPS):
+        if sweep == SWEEPS - 1:
+            load_pold.wait()
+        def plane(x, sweep=sweep):
+            for y in range(0, cy, 32):
+                sweep_plane(sweep, x, y, 32)
+
+        planes(0, cx, 4, plane)
+        if sweep == SWEEPS - 1:
+            planes(0, cx // 2, 4, functools.partial(coarse_plane, 0))
+        add_halos(sweep)
+
     unit_rows = packed.shape[2]
 
     def unit_copy(part, peer):
@@ -409,7 +433,7 @@
             stage[part, peer] = packed[part, order[0, peer]]
             unit_copy(part, peer).start()
 
-        planes(1, ndev - 1, 6, one)
+        planes(1, ndev - 1, 14, one)
         one(ndev - 1)
         recv[part, pl.ds(me * unit_rows, unit_rows), :] = packed[part, order[0, me]]
 
@@ -418,7 +442,9 @@
         pltpu.make_async_copy(others, others, unit_recv.at[part]).wait()
 
     save_order.wait()
-    planes(0, cx // 2, 4, functools.partial(coarse_plane, 0))
+    coarse_plane(0, 0)
+    coarse_plane(0, cx // 2 - 1)
+    planes(1, cx // 2 - 1, 6, coarse_outer)
     ship(0)
     for way in range(2):
         receive(SWEEPS, way, lambda: None)

time: 49 us -> 49 us (level)
  no operation moved by 1% of the time
where the time goes in v4:
time: 49 us; the launch traced here: 48.9 us
  Pallas kernels  48.3 us (99%)
  between operations  0.64 us (1%)
    pallas_call x1, Pallas kernels, body(): pl.pallas_call(functools.partial(kernel_body, (ngx, ngy, cx, cy, cz, chun...  46 us
    pallas_call x1, Pallas kernels, body(): pl.pallas_call(functools.partial(output_body, cz), out_shape=(jax.ShapeDt...  2.31 us

profile of v4, /device:TPU:1, one launch (start us, length us, event | category | flops | bytes accessed | tf_op | source)
XLA Modules:
  0.0 48.9 jit_solution(3264961465286736380)
XLA Ops:
  0.6 46.0 %shard_map.86 = (f32[2,4096,128]{2,1,0:T(8,128)S(1)}, f32[3,128,512]{2,1,0:T(8,128)S(1)}, f32[2,1024,128]{2,1,0:T(8,128)S(1)}) custom-call(s32[1,128]{1,0:T(1,128)} %bitcast.12, f32[2,4096,128]{2,1,0:T(8,128)} %bitcast.7, f32[4096,128]{1,0:T(8,128)} %bitcast.8, f32[4096,128]{1,0:T(8,128)} %bitcast.9, f32[4096,128]{1,0:T(8,128)} %bitcast.10, ...), custom_call_target="tpu_custom_call" | custom-call | tf_op jit(solution)/shard_map/pallas_call | solution.py:513
  46.6 2.3 %shard_map.87 = (f32[2,4096,128]{2,1,0:T(8,128)}, f32[3,128,512]{2,1,0:T(8,128)}) custom-call(f32[2,4096,128]{2,1,0:T(8,128)S(1)} %get-tuple-element.7.corr, f32[3,128,512]{2,1,0:T(8,128)S(1)} %get-tuple-element.8.mom, f32[2,1024,128]{2,1,0:T(8,128)S(1)} %get-tuple-element.9.recv), custom_call_target="tpu_custom_call" | custom-call | tf_op jit(solution)/shard_map/pallas_call | solution.py:566

commit v5 on v3

--- a/solution.py
+++ b/solution.py
@@ -316,7 +316,6 @@
                 for c in range(2):
                     more = inv[c, plain(x), :] * x_recv[sweep, side, c]
                     if last:
-                        corr[c, plain(x), :] += scales[3] * more
                         if c == 0:
                             phase[padded(x), :] += scales[3] * more
                     else:
@@ -330,7 +329,6 @@
                 for c in range(2):
                     more = inv_edge[side, c] * y_recv[sweep, side, c]
                     if last:
-                        corr[c, plain_column(y), :] += scales[3] * more
                         if c == 0:
                             phase[padded_column(y), :] += scales[3] * more
                     else:
@@ -345,6 +343,21 @@
                 for c in range(2):
                     y_send[sweep + 1, side, c] = into[c, padded_column(ends_y[side]), :]
         send(sweep + 1, (2, 3))
+        for side in range(2) if last else ():
+
+            @pl.when(sends[side])
+            def _(side=side):
+                at = plain(ends_x[side])
+                for c in range(2):
+                    corr[c, at, :] += scales[3] * (inv[c, at, :] * x_recv[sweep, side, c])
+
+        for side in range(2) if last else ():
+
+            @pl.when(sends[2 + side])
+            def _(side=side):
+                at = plain_column(ends_y[side])
+                for c in range(2):
+                    corr[c, at, :] += scales[3] * (inv_edge[side, c] * y_recv[sweep, side, c])
 
     for sweep in range(SWEEPS):
         if sweep == SWEEPS - 1:

time: 49 us -> 49.1 us (level)
  no operation moved by 1% of the time
where the time goes in v5:
time: 49.1 us; the launch traced here: 49 us
  Pallas kernels  48.4 us (99%)
  between operations  0.64 us (1%)
    pallas_call x1, Pallas kernels, body(): pl.pallas_call(functools.partial(kernel_body, (ngx, ngy, cx, cy, cz, chun...  46.1 us
    pallas_call x1, Pallas kernels, body(): pl.pallas_call(functools.partial(output_body, cz), out_shape=(jax.ShapeDt...  2.31 us

profile of v5, /device:TPU:1, one launch (start us, length us, event | category | flops | bytes accessed | tf_op | source)
XLA Modules:
  0.0 49.0 jit_solution(15177665581225885320)
XLA Ops:
  0.6 46.1 %shard_map.86 = (f32[2,4096,128]{2,1,0:T(8,128)S(1)}, f32[3,128,512]{2,1,0:T(8,128)S(1)}, f32[2,1024,128]{2,1,0:T(8,128)S(1)}) custom-call(s32[1,128]{1,0:T(1,128)} %bitcast.12, f32[2,4096,128]{2,1,0:T(8,128)} %bitcast.7, f32[4096,128]{1,0:T(8,128)} %bitcast.8, f32[4096,128]{1,0:T(8,128)} %bitcast.9, f32[4096,128]{1,0:T(8,128)} %bitcast.10, ...), custom_call_target="tpu_custom_call" | custom-call | tf_op jit(solution)/shard_map/pallas_call | solution.py:500
  46.7 2.3 %shard_map.87 = (f32[2,4096,128]{2,1,0:T(8,128)}, f32[3,128,512]{2,1,0:T(8,128)}) custom-call(f32[2,4096,128]{2,1,0:T(8,128)S(1)} %get-tuple-element.7.corr, f32[3,128,512]{2,1,0:T(8,128)S(1)} %get-tuple-element.8.mom, f32[2,1024,128]{2,1,0:T(8,128)S(1)} %get-tuple-element.9.recv), custom_call_target="tpu_custom_call" | custom-call | tf_op jit(solution)/shard_map/pallas_call | solution.py:553
